TPU v7x, 256 devices: a whole 4x4x8 slice. The times are simulated.
256 devices in a mesh: dish: 8 (over y, x_hi), blk: 32 (over x_lo, z, core).
Axes of the slice: x: 4 (x_hi: 2, x_lo: 2; x = x_hi * 2 + x_lo), y: 4, z: 8, core: 2. Of those that a mesh axis runs over, the one named last changes fastest.
Arguments:
- sky_data: float32 [8, 2048, 32768], P('dish', 'blk'), may hold values from -6 to 6
- eigenmodes: float32 [2048, 64], replicated, may hold values from -0.125 to 0.125
- noise_power: float32 [64, 32768], P('blk'), may hold values from 0.1 to 10
Outputs:
- cleaned: bfloat16 [8, 2048, 32768], P('dish', 'blk')
- mode_signal: float32 [8, 64, 32768], P('dish', 'blk')
All inputs are finite; a program needn't handle non-finite values.
Results may differ from a plain program's by a relative error of at most 0.0028.
Values may be sent and summed in bfloat16 or wider, within the bound.
No kernel may reach another device: no remote copies, remote signals or barrier semaphores. Data moves between devices by JAX's collectives and lax.ppermute only.
A program may use at most 128 MiB of HBM per device.

v0:
```python
import math
import jax
import jax.numpy as jnp
from jax import lax
from jax.sharding import Mesh
from jax.sharding import PartitionSpec as P

BLK = ("blk_0", "blk_1", "blk_2")
highest = lax.Precision.HIGHEST


def sent_to_all(value, axis):
    copies = jnp.broadcast_to(value, (lax.axis_size(axis), *value.shape))
    return lax.all_to_all(copies, axis, split_axis=0, concat_axis=0, tiled=True)


def taken_together(value, axis):
    return sent_to_all(value, axis).astype(jnp.float32).sum(axis=0)


def in_blocks(value, dim, size):
    before, after = (value.shape[:dim], value.shape[dim + 1 :])
    return jnp.moveaxis(value.reshape(*before, size, -1, *after), dim, 0)


def sent_and_summed(value, axis, dim):
    size = lax.axis_size(axis)
    parts = lax.all_to_all(in_blocks(value, dim, size), axis, 0, 0, tiled=True)
    return jnp.sum(parts, axis=0)


def sum_by_axis(value, axes, dim):
    far, near = axes
    parts = in_blocks(value, dim, lax.axis_size(far))
    nearer = sent_and_summed(parts, near, dim + 1)
    arrived = lax.all_to_all(nearer, far, split_axis=0, concat_axis=0, tiled=True)
    return arrived.sum(axis=0)


def dft_table(length):
    index = jnp.arange(length, dtype=jnp.int32)
    phase = (index[:, None] * index[None, :] % length).astype(jnp.float32) * (
        2.0 * math.pi / length
    )
    return (jnp.cos(phase), jnp.sin(phase))


def twist_table(rows_count, cols_count):
    total = rows_count * cols_count
    first = jnp.arange(rows_count, dtype=jnp.int32)
    second = jnp.arange(cols_count, dtype=jnp.int32)
    phase = (first[:, None] * second[None, :] % total).astype(jnp.float32) * (2.0 * math.pi / total)
    return (jnp.cos(phase), jnp.sin(phase))


def forward(series, tables):
    col_cos, col_sin, row_cos, row_sin, twist_cos, twist_sin = tables
    batch_count, length = series.shape
    grid = series.reshape(batch_count, length // 128, 128)
    inner_real = jnp.einsum("bqp,qk->bpk", grid, col_cos, precision=highest)
    inner_imag = -jnp.einsum("bqp,qk->bpk", grid, col_sin, precision=highest)
    turned_real = inner_real * twist_cos + inner_imag * twist_sin
    turned_imag = inner_imag * twist_cos - inner_real * twist_sin
    spec_real = jnp.einsum("kp,bpj->bkj", row_cos, turned_real, precision=highest) + jnp.einsum(
        "kp,bpj->bkj", row_sin, turned_imag, precision=highest
    )
    spec_imag = jnp.einsum("kp,bpj->bkj", row_cos, turned_imag, precision=highest) - jnp.einsum(
        "kp,bpj->bkj", row_sin, turned_real, precision=highest
    )
    return (spec_real, spec_imag)


def inverse(held_real, held_imag, tables, length):
    col_cos, col_sin, row_cos, row_sin, twist_cos, twist_sin = tables
    outer_real = jnp.einsum("pk,bkj->bpj", row_cos, held_real, precision=highest) - jnp.einsum(
        "pk,bkj->bpj", row_sin, held_imag, precision=highest
    )
    outer_imag = jnp.einsum("pk,bkj->bpj", row_cos, held_imag, precision=highest) + jnp.einsum(
        "pk,bkj->bpj", row_sin, held_real, precision=highest
    )
    back_real = outer_real * twist_cos - outer_imag * twist_sin
    back_imag = outer_real * twist_sin + outer_imag * twist_cos
    series = jnp.einsum("qk,bpk->bqp", col_cos, back_real, precision=highest) - jnp.einsum(
        "qk,bpk->bqp", col_sin, back_imag, precision=highest
    )
    return (series / length).reshape(held_real.shape[0], length)


def wiener(amplitude, noise_power):
    dish_local = amplitude.shape[0]
    owned_modes = amplitude.shape[1]
    length = amplitude.shape[2]
    columns = length // 128
    col_cos, col_sin = dft_table(columns)
    row_cos, row_sin = dft_table(128)
    twist_cos, twist_sin = twist_table(128, columns)
    tables = (col_cos, col_sin, row_cos, row_sin, twist_cos, twist_sin)
    spec_real, spec_imag = forward(amplitude.reshape(dish_local * owned_modes, length), tables)
    squared = spec_real * spec_real + spec_imag * spec_imag
    power_here = jnp.sum(squared.reshape(dish_local, owned_modes, 128, columns), axis=0)
    power_total = taken_together(power_here.astype(jnp.bfloat16), "dish").astype(jnp.float32)
    power = power_total / float(dish_local * lax.axis_size("dish") * length)
    gain = power / (power + noise_power.reshape(owned_modes, 128, columns))
    gain_rows = gain[None].reshape(dish_local * owned_modes, 128, columns)
    signal = inverse(spec_real * gain_rows, spec_imag * gain_rows, tables, length)
    return signal.reshape(dish_local, owned_modes, length)


def body(sky_data, eigenmodes, noise_power):
    channels = sky_data.shape[1]
    position = lax.axis_index(BLK)
    local_modes = lax.dynamic_slice_in_dim(eigenmodes, position * channels, channels, 0)
    picked = local_modes
    summed = sum_by_axis(
        jnp.einsum("cm,dct->mdt", picked, sky_data, precision=highest),
        (("blk_0", "blk_1"), "blk_2"),
        0,
    )
    owned_amplitude = jnp.transpose(summed, (1, 0, 2))
    signal = wiener(owned_amplitude, noise_power)
    picked = local_modes
    fitted = jnp.einsum(
        "cm,dmt->dct", picked, lax.all_gather(signal, BLK, axis=1, tiled=True), precision=highest
    )
    cleaned = (sky_data - fitted).astype(jnp.bfloat16)
    return (cleaned, signal)


def solution(mesh):
    finer = Mesh(
        mesh.devices.reshape(mesh.shape["dish"], 2, 8, 2), ("dish", "blk_0", "blk_1", "blk_2")
    )
    return jax.shard_map(
        body,
        mesh=finer,
        in_specs=(P("dish", BLK, None), P(), P(BLK, None)),
        out_specs=(P("dish", BLK, None), P("dish", BLK, None)),
        check_vma=False,
    )
```

profile of v0, /device:TPU:1, one launch (start us, length us, event | category | flops | bytes accessed | tf_op | source)
XLA Modules:
  0.0 277.2 jit_solution(2609861436061905775)
XLA Ops:
  7.2 0.0 copy-start
  7.2 1.0 copy-done
  8.2 0.1 constant_dynamic-slice_fusion
  8.3 10.1 %convolution_bitcast_fusion.1 = f32[2,16,2,1,32768]{4,1,2,3,0:T(8,128)S(1)} fusion(f32[1,64,32768]{2,1,0:T(8,128)} %param.3, f32[16,2,2,64]{3,2,1,0:T(2,128)S(1)} %bitcast.85), kind=kOutput, calls=%fused_computation.1 | convolution fusion | flops 1610612736 | bytes 16793600 | tf_op jit(solution)/shard_map/cm,dct->mdt/dot_general | solution.py:115
  18.4 13.3 %all_to_all.15 = f32[2,16,2,1,32768]{4,1,2,3,0:T(8,128)S(1)} all-to-all(f32[2,16,2,1,32768]{4,1,2,3,0:T(8,128)S(1)} %convolution_bitcast_fusion.1), channel_id=1, replica_groups=mesh['dish'=8,'blk_0'=2,'blk_1'=8,'blk_2'=2] {'blk_2'}, dimensions={0} | all-to-all | bytes 16777216 | tf_op jit(solution)/shard_map/all_to_all | solution.py:28
  31.7 0.7 bitcast_reduce_fusion
  32.5 5.2 %copy.49 = f32[16,2,1,32768]{3,1,2,0:T(2,128)} copy(f32[16,2,1,32768]{3,0,1,2:T(8,128)S(1)} %bitcast.82) | data formatting | bytes 8388608 | tf_op jit(solution)/shard_map/reduce_sum | solution.py:29
  37.7 7.6 %all-to-all-start.1 = ((f32[16,2,1,32768]{3,1,2,0:T(2,128)}), f32[16,2,1,32768]{3,1,2,0:T(2,128)}, u32[]{:S(2)}, u32[]{:S(2)}) async-start(f32[16,2,1,32768]{3,1,2,0:T(2,128)} %copy.49), calls=%async_computation.1 | async-start | bytes 8388608 | tf_op jit(solution)/shard_map/all_to_all | solution.py:36
  45.3 0.0 copy-start.1
  45.3 0.5 fusion.70
  45.8 94.2 %all-to-all-done.1 = f32[16,2,1,32768]{3,1,2,0:T(2,128)} async-done(((f32[16,2,1,32768]{3,1,2,0:T(2,128)}), f32[16,2,1,32768]{3,1,2,0:T(2,128)}, u32[]{:S(2)}, u32[]{:S(2)}) %all-to-all-start.1) | async-done | bytes 4194336 | tf_op jit(solution)/shard_map/all_to_all | solution.py:36
  140.0 3.6 %reduce_sum.35 = f32[2,32768]{1,0:T(2,128)S(1)} reduce(f32[16,2,1,32768]{3,1,2,0:T(2,128)} %all-to-all-done.1, f32[]{:T(128)} %constant.66.clone.1), dimensions={0,2}, to_apply=%region_1.0 | reduce | flops 983040 | bytes 4456452 | tf_op jit(solution)/shard_map/reduce_sum | solution.py:37
  143.6 1.5 convolution_negate_fusion
  145.1 1.5 fusion.15
  146.6 0.8 fusion.66
  147.3 0.8 fusion.64
  148.1 0.8 fusion.10
  148.9 0.8 add_convert_fusion
  149.7 0.1 copy.56
  149.8 1.1 broadcast_in_dim.2
  150.9 6.3 %all-to-all-start.2 = ((bf16[8,2,128,256]{3,2,1,0:T(8,128)(2,1)}), bf16[8,2,128,256]{3,2,1,0:T(8,128)(2,1)S(1)}, u32[]{:S(2)}, u32[]{:S(2)}) async-start(bf16[8,2,128,256]{3,2,1,0:T(8,128)(2,1)} %broadcast_in_dim.2), calls=%async_computation.2 | async-start | bytes 2097152 | tf_op jit(solution)/shard_map/all_to_all | solution.py:14
  157.2 0.3 all-gather.2.cloned.1.call-start
  157.5 0.0 copy-done.1
  157.5 0.1 copy.58
  157.6 14.9 %all-to-all-done.2 = bf16[8,2,128,256]{3,2,1,0:T(8,128)(2,1)S(1)} async-done(((bf16[8,2,128,256]{3,2,1,0:T(8,128)(2,1)}), bf16[8,2,128,256]{3,2,1,0:T(8,128)(2,1)S(1)}, u32[]{:S(2)}, u32[]{:S(2)}) %all-to-all-start.2) | async-done | bytes 1048608 | tf_op jit(solution)/shard_map/all_to_all | solution.py:14
  172.5 0.1 convert_reduce_fusion
  172.7 0.1 copy.57
  172.9 0.6 fusion.53
  173.5 0.6 fusion.49
  174.2 0.7 fusion.8
  174.8 0.7 fusion.7
  175.5 1.4 fusion.19
  176.9 1.4 fusion.6
  178.2 0.8 copy.63
  179.1 0.0 all-gather.2.cloned.1.call-update
  179.1 1.8 reshape_reshape.4
  180.9 70.9 %all-gather.2.cloned.1.call-done = f32[1,64,32768]{2,0,1:T(1,128)} async-done(((f32[1,2,32768]{2,0,1:T(1,128)}), f32[1,64,32768]{2,0,1:T(1,128)}) %all-gather.2.cloned.1.call-update) | async-done | bytes 8388624 | tf_op jit(solution)/shard_map/all_gather | solution.py:123
  251.9 18.5 %fusion.1 = bf16[1,64,32768]{2,1,0:T(8,128)(2,1)} fusion(f32[1,64,32768]{2,1,0:T(8,128)} %param.3, f32[64,64]{0,1:T(8,128)S(1)} %constant_dynamic-slice_fusion, f32[1,64,32768]{2,0,1:T(1,128)} %all-gather.2.cloned.1.call-done), kind=kOutput, calls=%fused_computation.3 | convolution fusion | flops 1614807040 | bytes 20987904 | tf_op jit(solution)/shard_map/cm,dmt->dct/dot_general | solution.py:122
  (2 shorter events, 0.1 us)
Async XLA Ops:
  7.2 1.0 copy-start
  37.7 102.3 %all-to-all-start.1 = ((f32[16,2,1,32768]{3,1,2,0:T(2,128)}), f32[16,2,1,32768]{3,1,2,0:T(2,128)}, u32[]{:S(2)}, u32[]{:S(2)}) async-start(f32[16,2,1,32768]{3,1,2,0:T(2,128)} %copy.49), calls=%async_computation.1 | async-start | bytes 8388608 | tf_op jit(solution)/shard_map/all_to_all | solution.py:36
  45.3 112.2 %copy-start.1 = (f32[2,32768]{1,0:T(2,128)S(1)}, f32[2,32768]{1,0:T(2,128)}, u32[]{:S(2)}) copy-start(f32[2,32768]{1,0:T(2,128)} %param.5) | copy-start | bytes 786436
  150.9 21.7 %all-to-all-start.2 = ((bf16[8,2,128,256]{3,2,1,0:T(8,128)(2,1)}), bf16[8,2,128,256]{3,2,1,0:T(8,128)(2,1)S(1)}, u32[]{:S(2)}, u32[]{:S(2)}) async-start(bf16[8,2,128,256]{3,2,1,0:T(8,128)(2,1)} %broadcast_in_dim.2), calls=%async_computation.2 | async-start | bytes 2097152 | tf_op jit(solution)/shard_map/all_to_all | solution.py:14
  157.2 94.7 %all-gather.2.cloned.1.call-start = ((), (), s32[]{:S(2)}) async-start(), calls=%async_computation.3 | async-start | bytes 8650752 | tf_op jit(solution)/shard_map/all_gather | solution.py:123
Sparse Core Ops, SparseCore 0:
  179.2 72.5 all-gather.1
where the time goes:
time: 278 us; the launch traced here: 277 us
  waiting for transfers between devices  180 us (65%)
  matrix products  40 us (14%)
  starting transfers between devices  14.2 us (5%)
  between operations  14.2 us (5%)
  blocking collectives  13.3 us (5%)
  local copies, waits for them, and re-layouts  10.5 us (4%)
  other arithmetic  5.01 us (2%)
    all_to_all x1, waiting for transfers between devices, sum_by_axis(): lax.all_to_all(nearer, far, split_axis=0, concat_axis=0, tiled=True)  94.2 us
    all_gather x1, waiting for transfers between devices, body(): lax.all_gather(signal, BLK, axis=1, tiled=True)  70.9 us
    dot_general x1, matrix products, body(): jnp.einsum('cm,dmt->dct', picked, lax.all_gather(signal, BLK, axis=1, til...  18.5 us
    all_to_all x1, waiting for transfers between devices, sent_to_all(): return lax.all_to_all(copies, axis, split_axis=0, concat_axis=0, tiled=True)  14.9 us
    all_to_all x1, blocking collectives, sent_and_summed(): parts = lax.all_to_all(in_blocks(value, dim, size), axis, 0, 0, tiled=True)  13.3 us
    dot_general x1, matrix products, body(): jnp.einsum('cm,dct->mdt', picked, sky_data, precision=highest)  10.1 us
    all_to_all x1, starting transfers between devices, sum_by_axis(): lax.all_to_all(nearer, far, split_axis=0, concat_axis=0, tiled=True)  7.58 us
    all_to_all x1, starting transfers between devices, sent_to_all(): return lax.all_to_all(copies, axis, split_axis=0, concat_axis=0, tiled=True)  6.33 us
  transfers between devices with their start and end apart: 3, of which 3 were waited for; matrix products, arithmetic and copies ran while one was open for 1% of the time, Pallas kernels for 0%

commit v1 on v0

--- a/solution.py
+++ b/solution.py
@@ -120,7 +120,12 @@
     signal = wiener(owned_amplitude, noise_power)
     picked = local_modes
     fitted = jnp.einsum(
-        "cm,dmt->dct", picked, lax.all_gather(signal, BLK, axis=1, tiled=True), precision=highest
+        "cm,dmt->dct",
+        picked,
+        jnp.concatenate(
+            lax.all_to_all(jnp.stack([signal] * lax.axis_size(BLK)), BLK, 0, 0), axis=1
+        ),
+        precision=highest,
     )
     cleaned = (sky_data - fitted).astype(jnp.bfloat16)
     return (cleaned, signal)

time: 278 us -> 400 us (1.44)
  waiting for transfers between devices: 180 us -> 293 us
  local copies, waits for them, and re-layouts: 10.5 us -> 26.9 us
  between operations: 14.2 us -> 0.85 us
  starting transfers between devices: 14.2 us -> 25.1 us
  matrix products: 40 us -> 34.3 us
    all_to_all x0 -> x1, waiting for transfers between devices: none -> 183 us  [body(): lax.all_to_all(jnp.stack([signal] * lax.axis_size(BLK)), BLK, 0, 0)]
    all_gather x1 -> x0, waiting for transfers between devices: 70.9 us -> none  [body(): lax.all_gather(signal, BLK, axis=1, tiled=True)]
    another operation x0 -> x2, local copies, waits for them, and re-layouts: none -> 17.9 us
    all_to_all x0 -> x1, starting transfers between devices: none -> 11.1 us  [body(): lax.all_to_all(jnp.stack([signal] * lax.axis_size(BLK)), BLK, 0, 0)]
    dot_general x1, matrix products: 18.5 us -> 12.8 us  [body(): jnp.einsum('cm,dmt->dct', picked, jnp.concatenate(lax.all_to_all(jnp.stac...]
  transfers between devices with their start and end apart: 3 -> 3, of which waited for: 3 -> 3; matrix products, arithmetic and copies ran while one was open for 1% -> 0% of each run, Pallas kernels for 0% -> 0%
where the time goes in v1:
time: 400 us; the launch traced here: 398 us
  waiting for transfers between devices  293 us (73%)
  matrix products  34.3 us (9%)
  local copies, waits for them, and re-layouts  26.9 us (7%)
  starting transfers between devices  25.1 us (6%)
  blocking collectives  13.3 us (3%)
  other arithmetic  5.01 us (1%)
    all_to_all x1, waiting for transfers between devices, body(): lax.all_to_all(jnp.stack([signal] * lax.axis_size(BLK)), BLK, 0, 0)  183 us
    all_to_all x1, waiting for transfers between devices, sum_by_axis(): lax.all_to_all(nearer, far, split_axis=0, concat_axis=0, tiled=True)  94.2 us
    all_to_all x1, waiting for transfers between devices, sent_to_all(): return lax.all_to_all(copies, axis, split_axis=0, concat_axis=0, tiled=True)  15.2 us
    all_to_all x1, blocking collectives, sent_and_summed(): parts = lax.all_to_all(in_blocks(value, dim, size), axis, 0, 0, tiled=True)  13.3 us
    dot_general x1, matrix products, body(): jnp.einsum('cm,dmt->dct', picked, jnp.concatenate(lax.all_to_all(jnp.stac...  12.8 us
    all_to_all x1, starting transfers between devices, body(): lax.all_to_all(jnp.stack([signal] * lax.axis_size(BLK)), BLK, 0, 0)  11.1 us
    another operation x1, local copies, waits for them, and re-layouts  10.9 us
    dot_general x1, matrix products, body(): jnp.einsum('cm,dct->mdt', picked, sky_data, precision=highest)  10.1 us
  transfers between devices with their start and end apart: 3, of which 3 were waited for; matrix products, arithmetic and copies ran while one was open for 0% of the time, Pallas kernels for 0%

profile of v1, /device:TPU:1, one launch (start us, length us, event | category | flops | bytes accessed | tf_op | source)
XLA Modules:
  0.0 397.9 jit_solution(13100780893684145278)
XLA Ops:
  0.6 0.0 copy-start
  0.7 1.0 copy-done
  1.7 0.1 constant_dynamic-slice_fusion
  1.8 10.1 %convolution_bitcast_fusion.1 = f32[2,16,2,1,32768]{4,1,2,3,0:T(8,128)S(1)} fusion(f32[1,64,32768]{2,1,0:T(8,128)} %param.3, f32[16,2,2,64]{3,2,1,0:T(2,128)S(1)} %bitcast.87), kind=kOutput, calls=%fused_computation.1 | convolution fusion | flops 1610612736 | bytes 16793600 | tf_op jit(solution)/shard_map/cm,dct->mdt/dot_general | solution.py:115
  11.9 13.3 %all_to_all.20 = f32[2,16,2,1,32768]{4,1,2,3,0:T(8,128)S(1)} all-to-all(f32[2,16,2,1,32768]{4,1,2,3,0:T(8,128)S(1)} %convolution_bitcast_fusion.1), channel_id=1, replica_groups=mesh['dish'=8,'blk_0'=2,'blk_1'=8,'blk_2'=2] {'blk_2'}, dimensions={0} | all-to-all | bytes 16777216 | tf_op jit(solution)/shard_map/all_to_all | solution.py:28
  25.2 0.7 bitcast_reduce_fusion
  25.9 5.2 %copy.50 = f32[16,2,1,32768]{3,1,2,0:T(2,128)} copy(f32[16,2,1,32768]{3,0,1,2:T(8,128)S(1)} %bitcast.83) | data formatting | bytes 8388608 | tf_op jit(solution)/shard_map/reduce_sum | solution.py:29
  31.2 7.6 %all-to-all-start.1 = ((f32[16,2,1,32768]{3,1,2,0:T(2,128)}), f32[16,2,1,32768]{3,1,2,0:T(2,128)}, u32[]{:S(2)}, u32[]{:S(2)}) async-start(f32[16,2,1,32768]{3,1,2,0:T(2,128)} %copy.50), calls=%async_computation.1 | async-start | bytes 8388608 | tf_op jit(solution)/shard_map/all_to_all | solution.py:36
  38.8 0.0 copy-start.2
  38.8 0.5 fusion.68
  39.3 94.2 %all-to-all-done.1 = f32[16,2,1,32768]{3,1,2,0:T(2,128)} async-done(((f32[16,2,1,32768]{3,1,2,0:T(2,128)}), f32[16,2,1,32768]{3,1,2,0:T(2,128)}, u32[]{:S(2)}, u32[]{:S(2)}) %all-to-all-start.1) | async-done | bytes 4194336 | tf_op jit(solution)/shard_map/all_to_all | solution.py:36
  133.5 3.6 reduce_sum.35
  137.1 1.5 convolution_negate_fusion
  138.5 1.5 fusion.13
  140.0 0.8 fusion.64
  140.8 0.8 fusion.62
  141.6 0.8 fusion.8
  142.3 0.8 add_convert_fusion
  143.1 0.1 copy.57
  143.2 1.1 broadcast_in_dim.2
  144.3 6.4 %all-to-all-start.2 = ((bf16[8,2,128,256]{3,2,1,0:T(8,128)(2,1)}), bf16[8,2,128,256]{3,2,1,0:T(8,128)(2,1)S(1)}, u32[]{:S(2)}, u32[]{:S(2)}) async-start(bf16[8,2,128,256]{3,2,1,0:T(8,128)(2,1)} %broadcast_in_dim.2), calls=%async_computation.2 | async-start | bytes 2097152 | tf_op jit(solution)/shard_map/all_to_all | solution.py:14
  150.7 0.0 copy-done.2
  150.7 0.1 copy.59
  150.8 15.2 %all-to-all-done.2 = bf16[8,2,128,256]{3,2,1,0:T(8,128)(2,1)S(1)} async-done(((bf16[8,2,128,256]{3,2,1,0:T(8,128)(2,1)}), bf16[8,2,128,256]{3,2,1,0:T(8,128)(2,1)S(1)}, u32[]{:S(2)}, u32[]{:S(2)}) %all-to-all-start.2) | async-done | bytes 1048608 | tf_op jit(solution)/shard_map/all_to_all | solution.py:14
  166.0 0.1 convert_reduce_fusion
  166.1 0.1 copy.58
  166.3 0.6 fusion.51
  167.0 0.6 fusion.47
  167.6 0.6 fusion.6
  168.3 0.6 fusion.5
  168.9 1.4 fusion.17
  170.3 1.4 fusion.4
  171.7 0.1 copy.64
  171.8 0.2 copy.92
  172.0 7.0 %stack.3 = f32[32,1,2,32768]{3,2,1,0:T(2,128)} broadcast(f32[2,32768]{1,0:T(2,128)S(1)} %bitcast.85), dimensions={2,3} | broadcast | bytes 8650752 | tf_op jit(solution)/shard_map/stack | solution.py:126
  179.0 11.1 %all-to-all-start.3 = ((f32[32,1,2,32768]{3,2,1,0:T(2,128)}), f32[32,1,2,32768]{3,2,1,0:T(2,128)}, u32[]{:S(2)}, u32[]{:S(2)}) async-start(f32[32,1,2,32768]{3,2,1,0:T(2,128)} %stack.3), calls=%async_computation.3 | async-start | bytes 16777216 | tf_op jit(solution)/shard_map/all_to_all | solution.py:126
  190.2 0.9 reshape_reshape.4
  191.0 183.2 %all-to-all-done.3 = f32[32,1,2,32768]{3,2,1,0:T(2,128)} async-done(((f32[32,1,2,32768]{3,2,1,0:T(2,128)}), f32[32,1,2,32768]{3,2,1,0:T(2,128)}, u32[]{:S(2)}, u32[]{:S(2)}) %all-to-all-start.3) | async-done | bytes 8388640 | tf_op jit(solution)/shard_map/all_to_all | solution.py:126
  374.2 10.9 %reshape.71 = f32[64,32768]{1,0:T(8,128)} reshape(f32[32,1,2,32768]{3,2,1,0:T(2,128)} %all-to-all-done.3) | data formatting | bytes 16777216 | tf_op jit(solution)/shard_map/reshape.10
  385.1 0.0 copy-start.1
  385.1 12.8 %fusion.1 = bf16[1,64,32768]{2,1,0:T(8,128)(2,1)} fusion(f32[1,64,32768]{2,1,0:T(8,128)} %param.3, f32[64,32768]{1,0:T(8,128)} %reshape.71, f32[64,64]{0,1:T(8,128)S(1)} %constant_dynamic-slice_fusion), kind=kOutput, calls=%fused_computation.3 | convolution fusion | flops 1614807040 | bytes 20987904 | tf_op jit(solution)/shard_map/cm,dmt->dct/dot_general | solution.py:122
  397.9 0.0 copy-done.1
  (2 shorter events, 0.1 us)
Async XLA Ops:
  0.6 1.1 copy-start
  31.2 102.3 %all-to-all-start.1 = ((f32[16,2,1,32768]{3,1,2,0:T(2,128)}), f32[16,2,1,32768]{3,1,2,0:T(2,128)}, u32[]{:S(2)}, u32[]{:S(2)}) async-start(f32[16,2,1,32768]{3,1,2,0:T(2,128)} %copy.50), calls=%async_computation.1 | async-start | bytes 8388608 | tf_op jit(solution)/shard_map/all_to_all | solution.py:36
  38.8 111.9 %copy-start.2 = (f32[2,32768]{1,0:T(2,128)S(1)}, f32[2,32768]{1,0:T(2,128)}, u32[]{:S(2)}) copy-start(f32[2,32768]{1,0:T(2,128)} %param.5) | copy-start | bytes 786436
  144.3 21.7 %all-to-all-start.2 = ((bf16[8,2,128,256]{3,2,1,0:T(8,128)(2,1)}), bf16[8,2,128,256]{3,2,1,0:T(8,128)(2,1)S(1)}, u32[]{:S(2)}, u32[]{:S(2)}) async-start(bf16[8,2,128,256]{3,2,1,0:T(8,128)(2,1)} %broadcast_in_dim.2), calls=%async_computation.2 | async-start | bytes 2097152 | tf_op jit(solution)/shard_map/all_to_all | solution.py:14
  179.0 195.2 %all-to-all-start.3 = ((f32[32,1,2,32768]{3,2,1,0:T(2,128)}), f32[32,1,2,32768]{3,2,1,0:T(2,128)}, u32[]{:S(2)}, u32[]{:S(2)}) async-start(f32[32,1,2,32768]{3,2,1,0:T(2,128)} %stack.3), calls=%async_computation.3 | async-start | bytes 16777216 | tf_op jit(solution)/shard_map/all_to_all | solution.py:126
  385.1 12.8 %copy-start.1 = (f32[2048,64]{0,1:T(8,128)S(1)}, f32[2048,64]{0,1:T(8,128)}, u32[]{:S(2)}) copy-start(f32[2048,64]{0,1:T(8,128)} %param.4) | copy-start | bytes 1572868
